TPU v7x, 32 devices: a whole 2x2x4 slice. The times are simulated.
32 devices in a mesh: day: 2 (over core), region: 4 (over y, x), scen: 4 (over z).
Axes of the slice: x: 2, y: 2, z: 4, core: 2. Of those that a mesh axis runs over, the one named last changes fastest.
Arguments:
- shipments_init: float32 [4, 4, 4, 128, 2, 256], P('scen', 'region', None, None, 'day'), may hold values from 0 to 1
- holdings_init: float32 [4, 400, 2, 6, 256], P('scen', 'region', 'day'), may hold values from 0 to 2
- selling_init: float32 [4, 400, 2, 6, 256], P('scen', 'region', 'day'), may hold values from 0 to 1
- shortage_init: float32 [4, 400, 2, 256], P('scen', 'region', 'day'), may hold values from 0 to 1
- ordering_init: float32 [60, 256], P('region'), may hold values from 0 to 20
- balance_dual_init: float32 [4, 400, 2, 6, 256], P('scen', 'region', 'day'), may hold values from -3 to 3
- demand_dual_init: float32 [4, 400, 2, 256], P('scen', 'region', 'day'), may hold values from -3 to 3
- depot_dual_init: float32 [4, 60, 2, 256], P('scen', 'region', 'day'), may hold values from 0 to 0.1
- demand_base: float32 [400, 256], P('region'), may hold values from 0.5 to 2
- demand_pattern: float32 [16, 256], replicated, may hold values from 0.5 to 2
- demand_index: int32 [4, 400, 2], P('scen', 'region', 'day'), may hold values from 0 to 15
- initial_stock: float32 [400, 5, 256], P('region'), may hold values from 0 to 2
- depot_supply: float32 [60, 2, 256], P('region', 'day'), may hold values from 4 to 16
- lane_cost: float32 [4, 4, 128], replicated, may hold values from 0.1 to 1
- item_volume: float32 [256], replicated, may hold values from 0.5 to 2
- holding_cost: float32 [6, 256], replicated, may hold values from 0.05 to 0.5
- unit_price: float32 [256], replicated, may hold values from 1 to 4
- short_penalty: float32 [256], replicated, may hold values from 2 to 8
- order_cost: float32 [256], replicated, may hold values from 0.5 to 2
- lane_depot: int32 [4, 4, 128], replicated, may hold values from 0 to 14
- lane_store: int32 [4, 4, 128], replicated, may hold values from 0 to 99
- lane_mask: int32 [4, 4, 128], replicated, may hold values 0 or 1
Outputs:
- shipments: float32 [4, 4, 4, 128, 2, 256], P('scen', 'region', None, None, 'day')
- holdings: float32 [4, 400, 2, 6, 256], P('scen', 'region', 'day')
- selling: float32 [4, 400, 2, 6, 256], P('scen', 'region', 'day')
- ordering: float32 [60, 256], P('region')
- balance_dual: float32 [4, 400, 2, 6, 256], P('scen', 'region', 'day')
- depot_dual: float32 [4, 60, 2, 256], P('scen', 'region', 'day')
All inputs are finite; a program needn't handle non-finite values.
Results may differ from a plain program's by a relative error of at most 0.0003.
Values sent between devices are 32-bit elements; how exact they have to be, the bound alone decides.
A program may use at most 128 MiB of HBM per device.

v0:
```python
import jax
import jax.numpy as jnp
from jax import lax
from jax.sharding import PartitionSpec as P

ITERS = 4


primal_step = 0.25
order_step = 0.05
dual_step = 0.25
depot_step = 0.02


def carried_in(value, axis, combine, identity, reverse):
    peers, position = (lax.axis_size(axis), lax.axis_index(axis))
    everything = jax.tree.map(lambda part: lax.all_gather(part, axis), value)
    start = jax.tree.map(
        lambda part, zero: jnp.broadcast_to(jnp.asarray(zero, part.dtype), part.shape),
        value,
        identity,
    )

    def hop(k, before):
        at = peers - 1 - k if reverse else k
        reached = at > position if reverse else at < position
        new = combine(before, jax.tree.map(lambda part: part[at], everything))
        return jax.tree.map(lambda a, b: jnp.where(reached, a, b), new, before)

    return lax.fori_loop(0, peers, hop, start)


def link_days(first_part, second_part):
    return (
        first_part[0] + second_part[0],
        jnp.where(second_part[2] > 0, second_part[1], first_part[1]),
        jnp.maximum(first_part[2], second_part[2]),
    )


def per_device(
    shipments_init,
    holdings_init,
    selling_init,
    shortage_init,
    ordering_init,
    balance_dual_init,
    demand_dual_init,
    depot_dual_init,
    demand_base,
    demand_pattern,
    demand_index,
    initial_stock,
    depot_supply,
    lane_cost,
    item_volume,
    holding_cost,
    unit_price,
    short_penalty,
    order_cost,
    lane_depot,
    lane_store,
    lane_mask,
):
    highest = lax.Precision.HIGHEST
    region = lax.axis_index("region")
    shipments = shipments_init[0, 0]
    holdings = holdings_init[0]
    selling = selling_init[0]
    shortage = shortage_init[0]
    ordering = ordering_init
    balance_dual = balance_dual_init[0]
    demand_dual = demand_dual_init[0]
    depot_dual = depot_dual_init[0]
    store_count, day_count, age_count, item_count = holdings.shape
    depot_count = depot_dual.shape[0]
    lane_weight = lane_mask.astype(jnp.float32)
    store_table = (lane_store[..., None] == jnp.arange(store_count, dtype=jnp.int32)).astype(
        jnp.float32
    ) * lane_weight[..., None]
    depot_table = (lane_depot[..., None] == jnp.arange(depot_count, dtype=jnp.int32)).astype(
        jnp.float32
    ) * lane_weight[..., None]
    into_stores = lax.dynamic_index_in_dim(store_table, region, 1, keepdims=False)
    tile_depots = lax.dynamic_index_in_dim(depot_table, region, 0, keepdims=False)
    tile_weight = lax.dynamic_index_in_dim(lane_weight, region, 0, keepdims=False)
    tile_cost = lax.dynamic_index_in_dim(lane_cost, region, 0, keepdims=False)
    lane_price = tile_cost[:, :, None, None] * item_volume
    keep_lanes = tile_weight[:, :, None, None]
    pattern_count = demand_pattern.shape[0]
    pattern_table = (
        demand_index[0][..., None] == jnp.arange(pattern_count, dtype=jnp.int32)
    ).astype(jnp.float32)
    demand = (
        jnp.einsum("sdp,pk->sdk", pattern_table, demand_pattern, precision=highest)
        * demand_base[:, None, :]
    )
    present = jnp.ones((), jnp.float32)
    nothing = (
        jnp.zeros((depot_count, item_count), jnp.float32),
        jnp.zeros((store_count, age_count - 1, item_count), jnp.float32),
        jnp.zeros((), jnp.float32),
    )
    for iterate in range(ITERS):
        depot_block = jnp.sum(depot_dual, axis=1)
        depot_later, ahead_first, seen_later = carried_in(
            (depot_block, balance_dual[:, 0, 1:, :], present), "day", link_days, nothing, True
        )
        order_total = lax.psum(depot_block, ("day", "scen"))
        depot_after = jnp.flip(jnp.cumsum(jnp.flip(depot_dual, 1), 1), 1) + depot_later[:, None, :]
        first_age = balance_dual[:, :, 0, :]
        store_lanes = jnp.einsum("alj,jtk->altk", into_stores, first_age, precision=highest)
        store_lanes = lax.all_to_all(store_lanes, "region", split_axis=0, concat_axis=0, tiled=True)
        depot_lanes = jnp.einsum("ald,dtk->altk", tile_depots, depot_after, precision=highest)
        next_dual = jnp.concatenate([balance_dual[:, 1:, 1:, :], ahead_first[:, None]], axis=1)
        next_dual = jnp.pad(next_dual, ((0, 0), (0, 0), (0, 1), (0, 0)))
        new_ship = keep_lanes * jnp.maximum(
            0.0, shipments - primal_step * (lane_price + store_lanes + depot_lanes)
        )
        new_hold = jnp.maximum(
            0.0, holdings - primal_step * (holding_cost - balance_dual + next_dual)
        )
        new_sell = jnp.maximum(
            0.0, selling - primal_step * (-unit_price - balance_dual - demand_dual[:, :, None, :])
        )
        new_short = jnp.maximum(0.0, shortage - primal_step * (short_penalty - demand_dual))
        new_order = jnp.maximum(0.0, ordering - order_step * (order_cost - order_total))
        ship_bar = 2.0 * new_ship - shipments
        hold_bar = 2.0 * new_hold - holdings
        sell_bar = 2.0 * new_sell - selling
        short_bar = 2.0 * new_short - shortage
        order_bar = 2.0 * new_order - ordering
        shipments, holdings, selling, shortage, ordering = (
            new_ship,
            new_hold,
            new_sell,
            new_short,
            new_order,
        )
        outflow = jnp.einsum("ald,altk->dtk", tile_depots, ship_bar, precision=highest)
        arrived = lax.all_to_all(ship_bar, "region", split_axis=0, concat_axis=0, tiled=True)
        arrivals = jnp.einsum("alj,altk->jtk", into_stores, arrived, precision=highest)
        net_flow = outflow - depot_supply
        net_before, last_before, seen_before = carried_in(
            (jnp.sum(net_flow, axis=1), hold_bar[:, -1, :-1, :], present),
            "day",
            link_days,
            nothing,
            False,
        )
        earliest = jnp.where(seen_before > 0, last_before, initial_stock)
        earlier = jnp.concatenate([earliest[:, None], hold_bar[:, :-1, :-1, :]], axis=1)
        carried = jnp.concatenate([arrivals[:, :, None, :], earlier], axis=2)
        balance_dual = balance_dual - dual_step * (hold_bar + sell_bar - carried)
        demand_dual = demand_dual + dual_step * (demand - jnp.sum(sell_bar, axis=2) - short_bar)
        running = jnp.cumsum(net_flow, axis=1) + net_before[:, None, :]
        depot_dual = jnp.maximum(0.0, depot_dual + depot_step * (running - order_bar[:, None, :]))
    return (
        shipments[None, None],
        holdings[None],
        selling[None],
        ordering,
        balance_dual[None],
        depot_dual[None],
    )


def solution(mesh):
    placed = (
        P("scen", "region", None, None, "day", None),
        P("scen", "region", "day", None, None),
        P("scen", "region", "day", None, None),
        P("scen", "region", "day", None),
        P("region", None),
        P("scen", "region", "day", None, None),
        P("scen", "region", "day", None),
        P("scen", "region", "day", None),
        P("region", None),
        P(),
        P("scen", "region", "day"),
        P("region", None, None),
        P("region", "day", None),
        P(),
        P(),
        P(),
        P(),
        P(),
        P(),
        P(),
        P(),
        P(),
    )
    return jax.shard_map(
        per_device,
        mesh=mesh,
        in_specs=placed,
        out_specs=(
            P("scen", "region", None, None, "day", None),
            P("scen", "region", "day", None, None),
            P("scen", "region", "day", None, None),
            P("region", None),
            P("scen", "region", "day", None, None),
            P("scen", "region", "day", None),
        ),
        check_vma=False,
    )
```

profile of v0, /device:TPU:1, one launch (start us, length us, event | category | flops | bytes accessed | tf_op | source)
XLA Modules:
  0.0 327.2 jit_solution(12086876726479881778)
XLA Ops:
  4.6 4.3 %all-to-all-start = ((f32[4,128,1,256]{3,1,2,0:T(8,128)}), f32[4,128,1,256]{3,1,2,0:T(8,128)}, u32[]{:S(2)}, u32[]{:S(2)}) async-start(f32[4,128,1,256]{3,1,2,0:T(8,128)} %convolution_bitcast_fusion.7), calls=%async_computation | async-start | bytes 1048576 | tf_op jit(solution)/shard_map/all_to_all | solution.py:113
  10.9 3.1 all-reduce.4
  14.5 2.5 all-gather.1
  19.6 3.5 %while.144 = (s32[]{:T(128)}, f32[15,256]{1,0:T(8,128)S(1)}, f32[100,5,256]{2,1,0:T(8,128)S(1)}, s32[]{:T(128)}, f32[2,15,256]{2,0,1:T(2,128)S(1)}, /*index=5*/f...) while((s32[]{:T(128)}, f32[15,256]{1,0:T(8,128)S(1)}, ...), condition=%wide.region_1.2_spmd.clone, body=%wide.region_0.1_spmd.clone.sunk | while | flops 395529 | bytes 1613007 | solution.py:30
  26.2 2.7 all-gather.3
  30.2 2.6 copy.239
  32.8 31.3 %psum.28 = f32[15,256]{1,0:T(8,128)} all-reduce(f32[15,256]{1,0:T(8,128)} %bitcast.539), channel_id=1, replica_groups=mesh['day'=2,'region'=4,'scen'=4] {'day','scen'}, use_global_device_ids=true, to_apply=%region_4.5 | all-reduce | flops 3840 | bytes 30720 | tf_op jit(solution)/shard_map/psum | solution.py:109
  72.6 7.0 %while.145 = (s32[]{:T(128)}, f32[15,256]{1,0:T(8,128)S(1)}, f32[100,5,256]{2,1,0:T(8,128)S(1)}, f32[]{:T(128)}, s32[]{:T(128)}, /*index=5*/f32[2,15,256]{2,1,0:...) while((s32[]{:T(128)}, f32[15,256]{1,0:T(8,128)S(1)}, ...), condition=%wide.region_3.4_spmd.clone, body=%wide.region_2.3_spmd.clone.sunk | while | flops 395527 | bytes 1582266 | solution.py:30
  79.7 4.2 %all-to-all-start.1 = ((f32[4,128,1,256]{3,1,2,0:T(8,128)}), f32[4,128,1,256]{3,1,2,0:T(8,128)}, u32[]{:S(2)}, u32[]{:S(2)}) async-start(f32[4,128,1,256]{3,1,2,0:T(8,128)} %fusion.70), calls=%async_computation.1 | async-start | bytes 1048576 | tf_op jit(solution)/shard_map/all_to_all | solution.py:141
  90.8 27.3 %psum.29 = f32[15,256]{1,0:T(8,128)} all-reduce(f32[15,256]{1,0:T(8,128)} %bitcast.536), channel_id=1, replica_groups=mesh['day'=2,'region'=4,'scen'=4] {'day','scen'}, use_global_device_ids=true, to_apply=%region_10.11 | all-reduce | flops 3840 | bytes 30720 | tf_op jit(solution)/shard_map/psum | solution.py:109
  120.5 3.5 %fusion.48 = (f32[100,256]{1,0:T(8,128)}, f32[100,1,6,256]{3,0,2,1:T(8,128)}, f32[100,1,6,256]{3,0,2,1:T(8,128)S(1)}) fusion(f32[100,256]{1,0:T(8,128)S(1)} %bitcast.532, f32[1,100,1,6,256]{4,2,3,1,0:T(1,128)} %param.43, f32[256]{0:T(256)} %copy-done.87, f32[1,100,1,6,256]{4,2,3,1,0:T(1,128)} %param.40, f32[100,256]{1,0:T(8,128)S(1)} %copy-done.59, ...), kind=kLoop, calls=%fused_computation.119 | loop fusion | flops 3046400 | bytes 3994624 | tf_op jit(solution)/shard_map/reduce_sum | solution.py:155
  126.0 3.4 %all-gather.5 = f32[200,1,5,256]{3,1,2,0:T(1,128)S(1)} all-gather(f32[100,1,5,256]{3,1,2,0:T(1,128)S(1)} %copy.181), channel_id=7, replica_groups=mesh['day'=2,'region'=4,'scen'=4] {'day'}, dimensions={0}, use_global_device_ids=true | all-gather | bytes 1536000 | tf_op jit(solution)/shard_map/all_gather | solution.py:17
  130.8 5.7 %while.146 = (s32[]{:T(128)}, f32[15,256]{1,0:T(8,128)S(1)}, f32[100,5,256]{2,1,0:T(8,128)S(1)}, s32[]{:T(128)}, f32[2,15,256]{2,1,0:T(8,128)S(1)}, /*index=5*/f...) while((s32[]{:T(128)}, f32[15,256]{1,0:T(8,128)S(1)}, ...), condition=%wide.region_6.7_spmd.clone, body=%wide.region_5.6_spmd.clone.sunk | while | flops 395529 | bytes 1582287 | solution.py:30
  140.2 3.9 %all-to-all-start.2 = ((f32[4,128,1,256]{3,1,2,0:T(8,128)}), f32[4,128,1,256]{3,1,2,0:T(8,128)S(1)}, u32[]{:S(2)}, u32[]{:S(2)}) async-start(f32[4,128,1,256]{3,1,2,0:T(8,128)} %convolution_bitcast_fusion.6), calls=%async_computation.2 | async-start | bytes 1048576 | tf_op jit(solution)/shard_map/all_to_all | solution.py:113
  144.0 3.0 all-gather.7
  155.1 2.9 all-gather.6
  158.2 7.0 %while.147 = (s32[]{:T(128)}, f32[15,256]{1,0:T(8,128)S(1)}, f32[100,5,256]{2,1,0:T(8,128)S(1)}, f32[]{:T(128)}, s32[]{:T(128)}, /*index=5*/f32[2,15,256]{2,1,0:...) while((s32[]{:T(128)}, f32[15,256]{1,0:T(8,128)S(1)}, ...), condition=%wide.region_9.10_spmd.clone, body=%wide.region_8.9_spmd.clone.sunk | while | flops 395527 | bytes 1582266 | solution.py:30
  165.2 3.6 %all-to-all-start.3 = ((f32[4,128,1,256]{3,1,2,0:T(8,128)}), f32[4,128,1,256]{3,1,2,0:T(8,128)S(1)}, u32[]{:S(2)}, u32[]{:S(2)}) async-start(f32[4,128,1,256]{3,1,2,0:T(8,128)} %fusion.67), calls=%async_computation.3 | async-start | bytes 1048576 | tf_op jit(solution)/shard_map/all_to_all | solution.py:141
  175.8 29.0 %psum.30 = f32[15,256]{1,0:T(8,128)} all-reduce(f32[15,256]{1,0:T(8,128)} %bitcast.535), channel_id=1, replica_groups=mesh['day'=2,'region'=4,'scen'=4] {'day','scen'}, use_global_device_ids=true, to_apply=%region_16.17 | all-reduce | flops 3840 | bytes 30720 | tf_op jit(solution)/shard_map/psum | solution.py:109
  210.7 2.5 all-gather.9
  214.7 5.7 %while.148 = (s32[]{:T(128)}, f32[15,256]{1,0:T(8,128)S(1)}, f32[100,5,256]{2,1,0:T(8,128)S(1)}, s32[]{:T(128)}, f32[2,15,256]{2,1,0:T(8,128)S(1)}, /*index=5*/f...) while((s32[]{:T(128)}, f32[15,256]{1,0:T(8,128)S(1)}, ...), condition=%wide.region_12.13_spmd.clone, body=%wide.region_11.12_spmd.clone.sunk | while | flops 395529 | bytes 1582287 | solution.py:30
  220.4 4.2 %all-to-all-start.4 = ((f32[4,128,1,256]{3,1,2,0:T(8,128)}), f32[4,128,1,256]{3,1,2,0:T(8,128)}, u32[]{:S(2)}, u32[]{:S(2)}) async-start(f32[4,128,1,256]{3,1,2,0:T(8,128)} %convolution_bitcast_fusion.5), calls=%async_computation.4 | async-start | bytes 1048576 | tf_op jit(solution)/shard_map/all_to_all | solution.py:113
  236.4 4.2 %all-to-all-start.5 = ((f32[4,128,1,256]{3,1,2,0:T(8,128)}), f32[4,128,1,256]{3,1,2,0:T(8,128)}, u32[]{:S(2)}, u32[]{:S(2)}) async-start(f32[4,128,1,256]{3,1,2,0:T(8,128)} %fusion.68), calls=%async_computation.5 | async-start | bytes 1048576 | tf_op jit(solution)/shard_map/all_to_all | solution.py:141
  243.0 4.7 %while.149 = (s32[]{:T(128)}, f32[15,256]{1,0:T(8,128)S(1)}, f32[100,5,256]{2,1,0:T(8,128)S(1)}, f32[]{:T(128)}, s32[]{:T(128)}, /*index=5*/f32[2,15,256]{2,1,0:...) while((s32[]{:T(128)}, f32[15,256]{1,0:T(8,128)S(1)}, ...), condition=%wide.region_15.16_spmd.clone, body=%wide.region_14.15_spmd.clone.sunk | while | flops 395527 | bytes 1582266 | solution.py:30
  249.9 26.9 %psum.31 = f32[15,256]{1,0:T(8,128)} all-reduce(f32[15,256]{1,0:T(8,128)S(1)} %bitcast.534), channel_id=1, replica_groups=mesh['day'=2,'region'=4,'scen'=4] {'day','scen'}, use_global_device_ids=true, to_apply=%region_20.21 | all-reduce | flops 3840 | bytes 30720 | tf_op jit(solution)/shard_map/psum | solution.py:109
  282.9 3.5 %all-gather.13 = f32[200,1,5,256]{3,1,2,0:T(1,128)S(1)} all-gather(f32[100,1,5,256]{3,1,2,0:T(1,128)S(1)} %copy.209), channel_id=15, replica_groups=mesh['day'=2,'region'=4,'scen'=4] {'day'}, dimensions={0}, use_global_device_ids=true | all-gather | bytes 1536000 | tf_op jit(solution)/shard_map/all_gather | solution.py:17
  287.6 3.4 %while.150 = (s32[]{:T(128)}, f32[15,256]{1,0:T(8,128)S(1)}, f32[100,5,256]{2,1,0:T(8,128)S(1)}, s32[]{:T(128)}, f32[2,15,256]{2,1,0:T(8,128)S(1)}, /*index=5*/f...) while((s32[]{:T(128)}, f32[15,256]{1,0:T(8,128)S(1)}, ...), condition=%wide.region_18.19_spmd.clone, body=%wide.region_17.18_spmd.clone.sunk | while | flops 395529 | bytes 1582287 | solution.py:30
  291.5 3.9 %all-to-all-start.6 = ((f32[4,128,1,256]{3,1,2,0:T(8,128)}), f32[4,128,1,256]{3,1,2,0:T(8,128)S(1)}, u32[]{:S(2)}, u32[]{:S(2)}) async-start(f32[4,128,1,256]{3,1,2,0:T(8,128)} %convolution_bitcast_fusion.4), calls=%async_computation.6 | async-start | bytes 1048576 | tf_op jit(solution)/shard_map/all_to_all | solution.py:113
  296.6 2.8 all-gather.15
  305.7 4.2 %all-to-all-start.7 = ((f32[4,128,1,256]{3,1,2,0:T(8,128)}), f32[4,128,1,256]{3,1,2,0:T(8,128)}, u32[]{:S(2)}, u32[]{:S(2)}) async-start(f32[4,128,1,256]{3,1,2,0:T(8,128)} %fusion.69), calls=%async_computation.7 | async-start | bytes 1048576 | tf_op jit(solution)/shard_map/all_to_all | solution.py:141
  309.9 2.9 all-gather.14
  313.0 4.7 %while.151 = (s32[]{:T(128)}, f32[15,256]{1,0:T(8,128)S(1)}, f32[100,5,256]{2,1,0:T(8,128)S(1)}, f32[]{:T(128)}, s32[]{:T(128)}, /*index=5*/f32[2,15,256]{2,1,0:...) while((s32[]{:T(128)}, f32[15,256]{1,0:T(8,128)S(1)}, ...), condition=%wide.region_22.23_spmd.clone, body=%wide.region_21.22_spmd.clone.sunk | while | flops 395527 | bytes 1582266 | solution.py:30
  (399 shorter events, 126.5 us)
Async XLA Ops:
  0.6 64.7 %copy-start = (f32[16,256]{1,0:T(8,128)S(1)}, f32[16,256]{1,0:T(8,128)}, u32[]{:S(2)}) copy-start(f32[16,256]{1,0:T(8,128)} %param.47) | copy-start | bytes 49156
  3.2 6.4 %copy-start.104 = (u32[32]{0:T(128)S(1)}, u32[32]{0:T(128)}, u32[]{:S(2)}) copy-start(u32[32]{0:T(128)} %constant.369) | copy-start | bytes 388
  4.6 62.6 %all-to-all-start = ((f32[4,128,1,256]{3,1,2,0:T(8,128)}), f32[4,128,1,256]{3,1,2,0:T(8,128)}, u32[]{:S(2)}, u32[]{:S(2)}) async-start(f32[4,128,1,256]{3,1,2,0:T(8,128)} %convolution_bitcast_fusion.7), calls=%async_computation | async-start | bytes 1048576 | tf_op jit(solution)/shard_map/all_to_all | solution.py:113
  8.9 144.1 %copy-start.70 = (f32[1,4,128]{2,1,0:T(4,128)}, f32[1,4,128]{2,1,0:T(4,128)S(1)}, u32[]{:S(2)}) copy-start(f32[1,4,128]{2,1,0:T(4,128)S(1)} %constant_dynamic-slice_fusion.4) | copy-start | bytes 6148
  23.8 96.6 %copy-start.39 = (f32[1,100,1,256]{3,1,2,0:T(8,128)}, f32[1,100,1,256]{3,1,2,0:T(8,128)S(1)}, u32[]{:S(2)}) copy-start(f32[1,100,1,256]{3,1,2,0:T(8,128)S(1)} %copy.362) | copy-start | bytes 307204
  25.6 39.7 %copy-start.35 = (f32[100,256]{1,0:T(8,128)}, f32[100,256]{1,0:T(8,128)S(1)}, u32[]{:S(2)}) copy-start(f32[100,256]{1,0:T(8,128)S(1)} %get-tuple-element.1905) | copy-start | bytes 307204
  29.5 123.5 %copy-start.72 = (s32[1,4,128]{2,1,0:T(4,128)}, s32[1,4,128]{2,1,0:T(4,128)S(1)}, u32[]{:S(2)}) copy-start(s32[1,4,128]{2,1,0:T(4,128)S(1)} %constant_dynamic-slice_fusion.2) | copy-start | bytes 6148
  79.7 39.3 %all-to-all-start.1 = ((f32[4,128,1,256]{3,1,2,0:T(8,128)}), f32[4,128,1,256]{3,1,2,0:T(8,128)}, u32[]{:S(2)}, u32[]{:S(2)}) async-start(f32[4,128,1,256]{3,1,2,0:T(8,128)} %fusion.70), calls=%async_computation.1 | async-start | bytes 1048576 | tf_op jit(solution)/shard_map/all_to_all | solution.py:141
  83.8 36.7 %copy-start.59 = (f32[100,256]{1,0:T(8,128)S(1)}, f32[100,256]{1,0:T(8,128)}, u32[]{:S(2)}) copy-start(f32[100,256]{1,0:T(8,128)} %get-tuple-element.1906) | copy-start | bytes 307204
  124.0 5.4 %copy-start.19 = (f32[100,1,6,256]{3,0,2,1:T(8,128)}, f32[100,1,6,256]{3,0,2,1:T(8,128)S(1)}, u32[]{:S(2)}) copy-start(f32[100,1,6,256]{3,0,2,1:T(8,128)S(1)} %get-tuple-element.1894) | copy-start | bytes 1843204
  130.7 6.0 %copy-start.81 = (f32[6,256]{1,0:T(8,128)S(1)}, f32[6,256]{1,0:T(8,128)}, u32[]{:S(2)}) copy-start(f32[6,256]{1,0:T(8,128)} %param.53) | copy-start | bytes 18436
  136.5 7.5 %copy-start.99 = (f32[2]{0:T(128)}, f32[2]{0:T(128)S(1)}, u32[]{:S(2)}) copy-start(f32[2]{0:T(128)S(1)} %get-tuple-element.2553) | copy-start | bytes 28
  140.2 11.4 %all-to-all-start.2 = ((f32[4,128,1,256]{3,1,2,0:T(8,128)}), f32[4,128,1,256]{3,1,2,0:T(8,128)S(1)}, u32[]{:S(2)}, u32[]{:S(2)}) async-start(f32[4,128,1,256]{3,1,2,0:T(8,128)} %convolution_bitcast_fusion.6), calls=%async_computation.2 | async-start | bytes 1048576 | tf_op jit(solution)/shard_map/all_to_all | solution.py:113
  153.0 5.1 %copy-start.58 = (f32[15,256]{1,0:T(8,128)S(1)}, f32[15,256]{1,0:T(8,128)}, u32[]{:S(2)}) copy-start(f32[15,256]{1,0:T(8,128)} %custom-call.6) | copy-start | bytes 46084
  153.1 5.1 %copy-start.100 = (f32[2]{0:T(128)S(1)}, f32[2]{0:T(128)}, u32[]{:S(2)}) copy-start(f32[2]{0:T(128)} %copy-done.99) | copy-start | bytes 28
  165.2 39.6 %copy-start.22 = (f32[100,5,256]{2,0,1:T(8,128)S(1)}, f32[100,5,256]{2,0,1:T(8,128)}, u32[]{:S(2)}) copy-start(f32[100,5,256]{2,0,1:T(8,128)} %param.49) | copy-start | bytes 1536004
  165.2 40.6 %all-to-all-start.3 = ((f32[4,128,1,256]{3,1,2,0:T(8,128)}), f32[4,128,1,256]{3,1,2,0:T(8,128)S(1)}, u32[]{:S(2)}, u32[]{:S(2)}) async-start(f32[4,128,1,256]{3,1,2,0:T(8,128)} %fusion.67), calls=%async_computation.3 | async-start | bytes 1048576 | tf_op jit(solution)/shard_map/all_to_all | solution.py:141
  208.7 16.1 %copy-start.11 = (f32[100,1,6,256]{3,0,2,1:T(8,128)}, f32[100,1,6,256]{3,0,2,1:T(8,128)S(1)}, u32[]{:S(2)}) copy-start(f32[100,1,6,256]{3,0,2,1:T(8,128)S(1)} %get-tuple-element.1891) | copy-start | bytes 1843204
  220.4 12.6 %all-to-all-start.4 = ((f32[4,128,1,256]{3,1,2,0:T(8,128)}), f32[4,128,1,256]{3,1,2,0:T(8,128)}, u32[]{:S(2)}, u32[]{:S(2)}) async-start(f32[4,128,1,256]{3,1,2,0:T(8,128)} %convolution_bitcast_fusion.5), calls=%async_computation.4 | async-start | bytes 1048576 | tf_op jit(solution)/shard_map/all_to_all | solution.py:113
  235.1 7.9 %copy-start.55 = (f32[15,256]{1,0:T(8,128)S(1)}, f32[15,256]{1,0:T(8,128)}, u32[]{:S(2)}) copy-start(f32[15,256]{1,0:T(8,128)} %custom-call.10) | copy-start | bytes 46084
  236.4 40.7 %all-to-all-start.5 = ((f32[4,128,1,256]{3,1,2,0:T(8,128)}), f32[4,128,1,256]{3,1,2,0:T(8,128)}, u32[]{:S(2)}, u32[]{:S(2)}) async-start(f32[4,128,1,256]{3,1,2,0:T(8,128)} %fusion.68), calls=%async_computation.5 | async-start | bytes 1048576 | tf_op jit(solution)/shard_map/all_to_all | solution.py:141
  247.7 30.8 %copy-start.12 = (f32[100,1,6,256]{3,0,2,1:T(8,128)S(1)}, f32[100,1,6,256]{3,0,2,1:T(8,128)}, u32[]{:S(2)}) copy-start(f32[100,1,6,256]{3,0,2,1:T(8,128)} %copy-done.11) | copy-start | bytes 1843204
  247.7 30.8 %copy-start.17 = (f32[100,1,6,256]{3,0,2,1:T(8,128)S(1)}, f32[100,1,6,256]{3,0,2,1:T(8,128)}, u32[]{:S(2)}) copy-start(f32[100,1,6,256]{3,0,2,1:T(8,128)} %get-tuple-element.1893) | copy-start | bytes 1843204
  247.7 30.8 %copy-start.88 = (f32[256]{0:T(256)S(1)}, f32[256]{0:T(256)}, u32[]{:S(2)}) copy-start(f32[256]{0:T(256)} %copy-done.87) | copy-start | bytes 3076
  247.8 29.0 %copy-start.60 = (f32[15,1,256]{2,0,1:T(8,128)}, f32[15,1,256]{2,0,1:T(8,128)S(1)}, u32[]{:S(2)}) copy-start(f32[15,1,256]{2,0,1:T(8,128)S(1)} %fusion.148) | copy-start | bytes 46084
  291.5 11.4 %all-to-all-start.6 = ((f32[4,128,1,256]{3,1,2,0:T(8,128)}), f32[4,128,1,256]{3,1,2,0:T(8,128)S(1)}, u32[]{:S(2)}, u32[]{:S(2)}) async-start(f32[4,128,1,256]{3,1,2,0:T(8,128)} %convolution_bitcast_fusion.4), calls=%async_computation.6 | async-start | bytes 1048576 | tf_op jit(solution)/shard_map/all_to_all | solution.py:113
  304.4 8.6 %copy-start.57 = (f32[15,256]{1,0:T(8,128)S(1)}, f32[15,256]{1,0:T(8,128)}, u32[]{:S(2)}) copy-start(f32[15,256]{1,0:T(8,128)} %custom-call.14) | copy-start | bytes 46084
  304.4 8.6 %copy-start.103 = (f32[2]{0:T(128)S(1)}, f32[2]{0:T(128)}, u32[]{:S(2)}) copy-start(f32[2]{0:T(128)} %copy-done.102) | copy-start | bytes 28
  305.7 16.9 %all-to-all-start.7 = ((f32[4,128,1,256]{3,1,2,0:T(8,128)}), f32[4,128,1,256]{3,1,2,0:T(8,128)}, u32[]{:S(2)}, u32[]{:S(2)}) async-start(f32[4,128,1,256]{3,1,2,0:T(8,128)} %fusion.69), calls=%async_computation.7 | async-start | bytes 1048576 | tf_op jit(solution)/shard_map/all_to_all | solution.py:141
  313.0 8.6 %copy-start.23 = (f32[100,5,256]{2,0,1:T(8,128)S(1)}, f32[100,5,256]{2,0,1:T(8,128)}, u32[]{:S(2)}) copy-start(f32[100,5,256]{2,0,1:T(8,128)} %param.49) | copy-start | bytes 1536004
  319.0 5.0 %copy-start.47 = (f32[100,256]{1,0:T(8,128)S(1)}, f32[100,256]{1,0:T(8,128)}, u32[]{:S(2)}) copy-start(f32[100,256]{1,0:T(8,128)} %multiply_add_fusion.4) | copy-start | bytes 307204
  319.1 5.0 %copy-start.89 = (f32[256]{0:T(256)S(1)}, f32[256]{0:T(256)}, u32[]{:S(2)}) copy-start(f32[256]{0:T(256)} %copy-done.87) | copy-start | bytes 3076
  (81 other events, 209.3 us)
where the time goes:
time: 331 us; the launch traced here: 327 us
  blocking collectives  158 us (48%)
  local copies, waits for them, and re-layouts  48 us (15%)
  other arithmetic  45.1 us (14%)
  starting transfers between devices  32.3 us (10%)
  matrix products  21.3 us (6%)
  loops' own time  16.3 us (5%)
  waiting for transfers between devices  3.8 us (1%)
    psum x4, blocking collectives, per_device(): order_total = lax.psum(depot_block, ('day', 'scen'))  114 us
    all_gather x16, blocking collectives, carried_in(): everything = jax.tree.map(lambda part: lax.all_gather(part, axis), value)  40.6 us
    unnamed x230, local copies, waits for them, and re-layouts  26.5 us
    another operation x8, loops' own time, carried_in(): return lax.fori_loop(0, peers, hop, start)  16.3 us
    all_to_all x4, starting transfers between devices, per_device(): lax.all_to_all(ship_bar, 'region', split_axis=0, concat_axis=0, tiled=True)  16.2 us
    all_to_all x4, starting transfers between devices, per_device(): lax.all_to_all(store_lanes, 'region', split_axis=0, concat_axis=0, tiled=...  16.1 us
    select_n x32, other arithmetic, hop(): return jax.tree.map(lambda a, b: jnp.where(reached, a, b), new, before)  16 us
    dynamic_slice x18, local copies, waits for them, and re-layouts, hop(): new = combine(before, jax.tree.map(lambda part: part[at], everything))  9.46 us
  transfers between devices with their start and end apart: 8, of which 3 were waited for; matrix products, arithmetic and copies ran while one was open for 13% of the time, Pallas kernels for 0%

commit v1 on v0

v1 whole, which is shorter than its diff:
```python
import functools

import jax
import jax.numpy as jnp
from jax import lax
from jax.experimental import pallas as pl
from jax.experimental.pallas import tpu as pltpu
from jax.sharding import PartitionSpec as P

ITERS = 4

primal_step = 0.25
order_step = 0.05
dual_step = 0.25
depot_step = 0.02


def round_up(value, step):
    return (value + step - 1) // step * step


def split_bf16(value):
    high = value.astype(jnp.bfloat16)
    low = (value - high.astype(jnp.float32)).astype(jnp.bfloat16)
    return high, low


def dot(a, b):
    return jnp.dot(a, b, preferred_element_type=jnp.float32)


def kernel(
    sizes,
    ship_in,
    hold_in,
    sell_in,
    short_in,
    order_in,
    bal_in,
    dem_in,
    dep_in,
    base_in,
    pattern_in,
    index_in,
    stock_in,
    supply_in,
    cost_ref,
    volume_ref,
    hcost_ref,
    price_ref,
    penalty_ref,
    ocost_ref,
    ldepot_ref,
    lstore_ref,
    lmask_ref,
    ship_out,
    hold_out,
    sell_out,
    order_out,
    bal_out,
    dep_out,
    ship,
    hold,
    sell,
    bal,
    held_bar,
    short,
    dem,
    demand,
    base,
    pattern,
    index,
    stock,
    supply,
    order,
    dep,
    lane_price,
    keep,
    into_lanes,
    from_lanes,
    prices,
    bar_high,
    bar_low,
    flow_send,
    flow_recv,
    after,
    block,
    local_sem,
    part_send,
    part_recv,
    tile_send,
    tile_recv,
    flow_ssem,
    flow_rsem,
    after_ssem,
    after_rsem,
    block_ssem,
    block_rsem,
    out_local,
    out_psend,
    out_precv,
    out_tsend,
    out_trecv,
):
    D, R, S, stores, depots, lanes, ages, K = sizes
    SP = round_up(stores, 128)
    DP = round_up(depots, 8)
    day, region, scen = lax.axis_index("day"), lax.axis_index("region"), lax.axis_index("scen")

    def turn(position, offset, count):
        return lax.rem(position + offset + count, count)

    def part(which):
        return pl.ds(pl.multiple_of(which * K, K), K)

    def to_peer(src, dst, ssem, rsem, where):
        return pltpu.make_async_remote_copy(
            src_ref=src,
            dst_ref=dst,
            send_sem=ssem,
            recv_sem=rsem,
            device_id=where,
            device_id_type=pl.DeviceIdType.MESH,
        )

    moves = [
        (lambda k: dep_in.at[:, 0, k], lambda t: dep.at[t]),
        (lambda k: supply_in.at[:, 0, k], lambda t: supply.at[t]),
    ]
    for a in range(ages):
        moves.append((lambda k, a=a: bal_in.at[:, a, 0, k], lambda t, a=a: bal.at[t, a]))
    moves.append((lambda k: dem_in.at[:, 0, k], lambda t: dem.at[t]))
    for a in range(ages):
        moves.append((lambda k, a=a: hold_in.at[:, a, 0, k], lambda t, a=a: hold.at[t, a]))
    for a in range(ages):
        moves.append((lambda k, a=a: sell_in.at[:, a, 0, k], lambda t, a=a: sell.at[t, a]))
    moves.append((lambda k: short_in.at[:, 0, k], lambda t: short.at[t]))
    moves.append((lambda k: index_in, lambda t: index.at[t]))

    mine = part(day)
    started = []
    for i, (src, dst) in enumerate(moves):
        started.append(pltpu.make_async_copy(src(mine), dst(day), local_sem.at[i]))
    extra = [
        (order_in.at[:, mine], order),
        (base_in.at[:, mine], base),
        (pattern_in.at[:, mine], pattern),
        (stock_in.at[:, :, mine], stock),
    ]
    for i, (src, dst) in enumerate(extra):
        started.append(pltpu.make_async_copy(src, dst, local_sem.at[len(moves) + i]))

    def tile(a):
        return pl.ds(pl.multiple_of(a * lanes, lanes), lanes)

    started.append(
        pltpu.make_async_copy(
            ship_in.at[tile(region), 0, mine],
            ship.at[tile(region), part(day)],
            local_sem.at[len(moves) + len(extra)],
        )
    )
    for copy in started:
        copy.start()

    barrier = pltpu.get_barrier_semaphore()
    count = 0
    for dc in range(D):
        for dr in range(R):
            if dc or dr:
                pl.semaphore_signal(
                    barrier,
                    inc=1,
                    device_id=(turn(day, dc, D), turn(region, dr, R), scen),
                    device_id_type=pl.DeviceIdType.MESH,
                )
                count += 1
    for ds in range(1, S):
        pl.semaphore_signal(
            barrier,
            inc=1,
            device_id=(day, region, turn(scen, ds, S)),
            device_id_type=pl.DeviceIdType.MESH,
        )
        count += 1
    pl.semaphore_wait(barrier, count)

    sends = []
    recvs = []

    def exchange(src_of, dst_of, ssem, rsem, dc, dr):
        to = (turn(day, dc, D), turn(region, dr, R), scen)
        out = to_peer(src_of(to[0], to[1]), dst_of(day, region), ssem, rsem, to)
        out.start()
        sends.append(out)
        back = (turn(day, -dc, D), turn(region, -dr, R), scen)
        return to_peer(src_of(to[0], to[1]), dst_of(back[0], back[1]), ssem, rsem, back)

    def ship_tiles(dc, dr):
        return exchange(
            lambda t, a: ship_in.at[tile(a), 0, part(t)],
            lambda t, a: ship.at[tile(a), part(t)],
            tile_send.at[dc, dr],
            tile_recv.at[dc, dr],
            dc,
            dr,
        )

    ship_recv = []
    for dr in range(1, R):
        for dc in range(D):
            ship_recv.append(ship_tiles(dc, dr))
    part_recvs = []
    for i, (src, dst) in enumerate(moves):
        for dc in range(1, D):
            part_recvs.append(
                exchange(
                    lambda t, a, src=src: src(part(t)),
                    lambda t, a, dst=dst: dst(t),
                    part_send.at[i, dc],
                    part_recv.at[i, dc],
                    dc,
                    0,
                )
            )
    for dc in range(1, D):
        ship_recv.append(ship_tiles(dc, 0))

    lane_ids = lax.broadcasted_iota(jnp.int32, (lanes, SP), 1).astype(jnp.float32)
    side_ids = lax.broadcasted_iota(jnp.int32, (lanes, R * DP), 1).astype(jnp.float32)
    store_ids = lax.broadcasted_iota(jnp.int32, (SP, lanes), 0).astype(jnp.float32)
    depot_ids = lax.broadcasted_iota(jnp.int32, (R * DP, lanes), 0).astype(jnp.float32)
    volume = volume_ref[:, mine]
    own = pl.ds(region, 1)
    for a in range(R):
        rows = slice(a * lanes, (a + 1) * lanes)
        store_row = lstore_ref[a, own, :].astype(jnp.float32)
        depot_row = ldepot_ref[a, own, :].astype(jnp.float32) + float(a * DP)
        weight_row = lmask_ref[a, own, :].astype(jnp.float32)
        cost_row = cost_ref[a, own, :]

        def column(row):
            return jnp.broadcast_to(row, (lanes, lanes)).T

        weight = column(weight_row)
        keep[rows, :] = weight[:, :K]
        lane_price[rows, :] = column(cost_row)[:, :1] * volume
        weight = weight[:, :1]
        into_lanes[rows, 0:SP] = jnp.where(
            lane_ids == column(store_row)[:, :1], weight, 0.0
        ).astype(jnp.bfloat16)
        into_lanes[rows, SP : SP + R * DP] = jnp.where(
            side_ids == column(depot_row)[:, :1], weight, 0.0
        ).astype(jnp.bfloat16)
        from_lanes[0:SP, rows] = jnp.where(store_ids == store_row, weight_row, 0.0).astype(
            jnp.bfloat16
        )
        from_lanes[SP : SP + R * DP, rows] = jnp.where(
            depot_ids == depot_row, weight_row, 0.0
        ).astype(jnp.bfloat16)
    prices[...] = jnp.zeros_like(prices)

    for copy in started:
        copy.wait()
    for copy in part_recvs[: 2 * (D - 1)]:
        copy.wait_recv()

    def send_after(it):
        total = dep[0]
        for t in range(1, D):
            total = total + dep[t]
        block[it, scen] = total
        later = dep[D - 1]
        after[it, region, D - 1] = later
        for t in reversed(range(D - 1)):
            later = later + dep[t]
            after[it, region, t] = later
        waits = []
        for dr in range(1, R):
            waits.append(
                exchange(
                    lambda t, a: after.at[it, region],
                    lambda t, a: after.at[it, a],
                    after_ssem.at[it, dr],
                    after_rsem.at[it, dr],
                    0,
                    dr,
                )
            )
        totals = []
        for ds in range(1, S):
            out = to_peer(
                block.at[it, scen],
                block.at[it, scen],
                block_ssem.at[it, ds],
                block_rsem.at[it, ds],
                (day, region, turn(scen, ds, S)),
            )
            out.start()
            sends.append(out)
            back = turn(scen, -ds, S)
            totals.append(
                to_peer(
                    block.at[it, back],
                    block.at[it, back],
                    block_ssem.at[it, ds],
                    block_rsem.at[it, ds],
                    (day, region, back),
                )
            )
        return waits, totals

    after_recv, block_recv = send_after(0)

    for copy in part_recvs[2 * (D - 1) :]:
        copy.wait_recv()

    pattern_ids = lax.broadcasted_iota(jnp.int32, (pattern.shape[0], stores), 0)
    table = pattern[...]
    for t in range(D):
        chosen = (pattern_ids == index[t]).astype(jnp.float32)
        demand[t] = (
            lax.dot_general(
                chosen,
                table,
                (((0,), (0,)), ((), ())),
                precision=lax.Precision.HIGHEST,
                preferred_element_type=jnp.float32,
            )
            * base[...]
        )

    hcost = hcost_ref[:, mine]
    unit_price = price_ref[:, mine]
    penalty = penalty_ref[:, mine]
    order_cost = ocost_ref[:, mine]

    def step_stores(t):
        price = dem[t]
        sold = jnp.zeros_like(price)
        for a in reversed(range(ages)):
            b, h, s = bal[t, a], hold[t, a], sell[t, a]
            slope = hcost[a : a + 1] - b
            if t + 1 < D and a + 1 < ages:
                slope = slope + bal[t + 1, a + 1]
            new_hold = jnp.maximum(0.0, h - primal_step * slope)
            new_sell = jnp.maximum(0.0, s - primal_step * (-unit_price - b - price))
            hold_bar = 2.0 * new_hold - h
            sell_bar = 2.0 * new_sell - s
            sold = sold + sell_bar
            change = hold_bar + sell_bar
            if a >= 1:
                change = change - (stock[a - 1] if t == 0 else held_bar[a - 1])
            bal[t, a] = b - dual_step * change
            hold[t, a] = new_hold
            sell[t, a] = new_sell
            held_bar[a] = hold_bar
        lost = short[t]
        new_short = jnp.maximum(0.0, lost - primal_step * (penalty - price))
        short[t] = new_short
        dem[t] = price + dual_step * (demand[t] - sold - (2.0 * new_short - lost))

    out_sends = []
    out_waits = []

    def put(i, array, out, t_ref):
        local = pltpu.make_async_copy(t_ref(day), out(mine), out_local.at[i])
        local.start()
        out_waits.append(local)
        for dc in range(1, D):
            to = (turn(day, dc, D), region, scen)
            go = to_peer(
                t_ref(to[0]), out(mine), out_psend.at[i, dc], out_precv.at[i, dc], to
            )
            go.start()
            out_sends.append(go)
            back = turn(day, -dc, D)
            recvs.append(
                to_peer(
                    t_ref(to[0]),
                    out(part(back)),
                    out_psend.at[i, dc],
                    out_precv.at[i, dc],
                    (back, region, scen),
                )
            )

    def put_ages(base_slot, array, out, which):
        for a in which:
            put(
                base_slot + a,
                array,
                lambda k, a=a: out.at[:, a, 0, k],
                lambda t, a=a: array.at[t, a],
            )

    for it in range(ITERS):
        final = it == ITERS - 1
        for t in range(D):
            prices[0:stores, t * K : (t + 1) * K] = bal[t, 0]
        early = D if it == 0 or final else 1
        for t in range(early):
            step_stores(t)
        if final:
            put_ages(0, hold, hold_out, range(ages))
            put_ages(ages, sell, sell_out, range(ages))
            put_ages(2 * ages, bal, bal_out, range(1, ages))
        if it == 0:
            for copy in ship_recv:
                copy.wait_recv()
        for copy in after_recv:
            copy.wait_recv()
        for a in range(R):
            for t in range(D):
                prices[SP + a * DP : SP + a * DP + depots, t * K : (t + 1) * K] = after[it, a, t]
        high, low = split_bf16(prices[...])
        for a in range(R):
            rows = slice(a * lanes, (a + 1) * lanes)
            spread = into_lanes[rows, :]
            cost = dot(spread, high) + dot(spread, low)
            for t in range(D):
                cols = slice(t * K, (t + 1) * K)
                old = ship[rows, cols]
                new = keep[rows, :] * jnp.maximum(
                    0.0, old - primal_step * (lane_price[rows, :] + cost[:, cols])
                )
                ship[rows, cols] = new
                bar = split_bf16(2.0 * new - old)
                bar_high[rows, cols] = bar[0]
                bar_low[rows, cols] = bar[1]
        gather = from_lanes[SP:, :]
        flow = dot(gather, bar_high[...]) + dot(gather, bar_low[...])
        for a in range(R):
            flow_send[it, a] = flow[a * DP : (a + 1) * DP, :]
        flow_waits = []
        for dr in range(1, R):
            flow_waits.append(
                exchange(
                    lambda t, a: flow_send.at[it, a],
                    lambda t, a: flow_recv.at[it, dr],
                    flow_ssem.at[it, dr],
                    flow_rsem.at[it, dr],
                    0,
                    dr,
                )
            )
        if final:
            for dr in list(range(1, R)) + [0]:
                for dc in range(D):
                    if dc == 0 and dr == 0:
                        local = pltpu.make_async_copy(
                            ship.at[tile(region), part(day)],
                            ship_out.at[tile(region), 0, mine],
                            out_local.at[3 * ages],
                        )
                        local.start()
                        out_waits.append(local)
                        continue
                    recvs.append(
                        exchange(
                            lambda t, a: ship.at[tile(a), part(t)],
                            lambda t, a: ship_out.at[tile(a), 0, part(t)],
                            out_tsend.at[dc, dr],
                            out_trecv.at[dc, dr],
                            dc,
                            dr,
                        )
                    )
        for t in range(early, D):
            step_stores(t)
        gather = from_lanes[0:SP, :]
        arrivals = dot(gather, bar_high[...]) + dot(gather, bar_low[...])
        for t in range(D):
            bal[t, 0] = bal[t, 0] + dual_step * arrivals[0:stores, t * K : (t + 1) * K]
        if final:
            put_ages(2 * ages, bal, bal_out, range(1))
        for copy in block_recv:
            copy.wait_recv()
        total = block[it, 0]
        for n in range(1, S):
            total = total + block[it, n]
        old = order[...]
        new = jnp.maximum(0.0, old - order_step * (order_cost - total))
        order[...] = new
        order_bar = 2.0 * new - old
        if final:
            put(3 * ages + 1, order, lambda k: order_out.at[:, k], lambda t: order)
        for copy in flow_waits:
            copy.wait_recv()
        outflow = flow_send[it, region]
        for dr in range(1, R):
            outflow = outflow + flow_recv[it, dr]
        running = -order_bar
        for t in range(D):
            running = running + (outflow[0:depots, t * K : (t + 1) * K] - supply[t])
            dep[t] = jnp.maximum(0.0, dep[t] + depot_step * running)
        if final:
            put(3 * ages + 2, dep, lambda k: dep_out.at[:, 0, k], lambda t: dep.at[t])
        else:
            after_recv, block_recv = send_after(it + 1)

    for copy in recvs:
        copy.wait_recv()
    for copy in sends + out_sends:
        copy.wait_send()
    for copy in out_waits:
        copy.wait()


def per_device(
    D,
    R,
    S,
    shipments_init,
    holdings_init,
    selling_init,
    shortage_init,
    ordering_init,
    balance_dual_init,
    demand_dual_init,
    depot_dual_init,
    demand_base,
    demand_pattern,
    demand_index,
    initial_stock,
    depot_supply,
    lane_cost,
    item_volume,
    holding_cost,
    unit_price,
    short_penalty,
    order_cost,
    lane_depot,
    lane_store,
    lane_mask,
):
    _, stores, local_days, ages, items = holdings_init.shape
    assert local_days == 1 and items % D == 0
    depots = depot_dual_init.shape[1]
    lanes = shipments_init.shape[3]
    K = items // D
    f32 = jnp.float32
    SP = round_up(stores, 128)
    DP = round_up(depots, 8)
    any_ = pl.BlockSpec(memory_space=pl.ANY)
    vmem = pl.BlockSpec(memory_space=pltpu.VMEM)
    moved = 4 + 3 * ages + 1
    DMA = pltpu.SemaphoreType.DMA
    rows = R * lanes
    outs = pl.pallas_call(
        functools.partial(kernel, (D, R, S, stores, depots, lanes, ages, K)),
        out_shape=(
            jax.ShapeDtypeStruct((rows, 1, items), f32),
            jax.ShapeDtypeStruct((stores, ages, 1, items), f32),
            jax.ShapeDtypeStruct((stores, ages, 1, items), f32),
            jax.ShapeDtypeStruct((depots, items), f32),
            jax.ShapeDtypeStruct((stores, ages, 1, items), f32),
            jax.ShapeDtypeStruct((depots, 1, items), f32),
        ),
        in_specs=[any_] * 13 + [vmem] * 9,
        out_specs=(any_,) * 6,
        scratch_shapes=[
            pltpu.VMEM((rows, D * K), f32),
            pltpu.VMEM((D, ages, stores, K), f32),
            pltpu.VMEM((D, ages, stores, K), f32),
            pltpu.VMEM((D, ages, stores, K), f32),
            pltpu.VMEM((ages, stores, K), f32),
            pltpu.VMEM((D, stores, K), f32),
            pltpu.VMEM((D, stores, K), f32),
            pltpu.VMEM((D, stores, K), f32),
            pltpu.VMEM((stores, K), f32),
            pltpu.VMEM((demand_pattern.shape[0], K), f32),
            pltpu.VMEM((D, 1, stores), jnp.int32),
            pltpu.VMEM((ages - 1, stores, K), f32),
            pltpu.VMEM((D, depots, K), f32),
            pltpu.VMEM((depots, K), f32),
            pltpu.VMEM((D, depots, K), f32),
            pltpu.VMEM((rows, K), f32),
            pltpu.VMEM((rows, K), f32),
            pltpu.VMEM((rows, SP + R * DP), jnp.bfloat16),
            pltpu.VMEM((SP + R * DP, rows), jnp.bfloat16),
            pltpu.VMEM((SP + R * DP, D * K), f32),
            pltpu.VMEM((rows, D * K), jnp.bfloat16),
            pltpu.VMEM((rows, D * K), jnp.bfloat16),
            pltpu.VMEM((ITERS, R, DP, D * K), f32),
            pltpu.VMEM((ITERS, R, DP, D * K), f32),
            pltpu.VMEM((ITERS, R, D, depots, K), f32),
            pltpu.VMEM((ITERS, S, depots, K), f32),
            DMA((moved + 5,)),
            DMA((moved, D)),
            DMA((moved, D)),
            DMA((D, R)),
            DMA((D, R)),
            DMA((ITERS, R)),
            DMA((ITERS, R)),
            DMA((ITERS, R)),
            DMA((ITERS, R)),
            DMA((ITERS, S)),
            DMA((ITERS, S)),
            DMA((3 * ages + 3,)),
            DMA((3 * ages + 3, D)),
            DMA((3 * ages + 3, D)),
            DMA((D, R)),
            DMA((D, R)),
        ],
        compiler_params=pltpu.CompilerParams(collective_id=0, has_side_effects=True),
    )(
        shipments_init.reshape(rows, 1, items),
        holdings_init.reshape(stores, ages, 1, items),
        selling_init.reshape(stores, ages, 1, items),
        shortage_init.reshape(stores, 1, items),
        ordering_init,
        balance_dual_init.reshape(stores, ages, 1, items),
        demand_dual_init.reshape(stores, 1, items),
        depot_dual_init.reshape(depots, 1, items),
        demand_base,
        demand_pattern,
        demand_index.reshape(1, stores),
        jnp.transpose(initial_stock, (1, 0, 2)),
        depot_supply.reshape(depots, 1, items),
        lane_cost,
        item_volume.reshape(1, items),
        holding_cost,
        unit_price.reshape(1, items),
        short_penalty.reshape(1, items),
        order_cost.reshape(1, items),
        lane_depot,
        lane_store,
        lane_mask,
    )
    return (
        outs[0].reshape(shipments_init.shape),
        outs[1].reshape(holdings_init.shape),
        outs[2].reshape(holdings_init.shape),
        outs[3],
        outs[4].reshape(holdings_init.shape),
        outs[5].reshape(depot_dual_init.shape),
    )


def solution(mesh):
    placed = (
        P("scen", "region", None, None, "day", None),
        P("scen", "region", "day", None, None),
        P("scen", "region", "day", None, None),
        P("scen", "region", "day", None),
        P("region", None),
        P("scen", "region", "day", None, None),
        P("scen", "region", "day", None),
        P("scen", "region", "day", None),
        P("region", None),
        P(),
        P("scen", "region", "day"),
        P("region", None, None),
        P("region", "day", None),
        P(),
        P(),
        P(),
        P(),
        P(),
        P(),
        P(),
        P(),
        P(),
    )
    return jax.shard_map(
        functools.partial(
            per_device, mesh.shape["day"], mesh.shape["region"], mesh.shape["scen"]
        ),
        mesh=mesh,
        in_specs=placed,
        out_specs=(
            P("scen", "region", None, None, "day", None),
            P("scen", "region", "day", None, None),
            P("scen", "region", "day", None, None),
            P("region", None),
            P("scen", "region", "day", None, None),
            P("scen", "region", "day", None),
        ),
        check_vma=False,
    )
```

time: 331 us -> 53.7 us (0.16); the launches traced: 327 us -> 53.4 us
  blocking collectives: 158 us -> 0 us
  Pallas kernels: 0 us -> 46.3 us
  other arithmetic: 45.1 us -> 0 us
  local copies, waits for them, and re-layouts: 48 us -> 6.42 us
  starting transfers between devices: 32.3 us -> 0 us
  matrix products: 21.3 us -> 0 us
  loops' own time: 16.3 us -> 0 us
  waiting for transfers between devices: 3.8 us -> 0 us
    psum x4 -> x0, blocking collectives: 114 us -> none  [per_device(): order_total = lax.psum(depot_block, ('day', 'scen'))]
    pallas_call x0 -> x1, Pallas kernels: none -> 46.3 us  [per_device(): pl.pallas_call(functools.partial(kernel, (D, R, S, stores, depots, lanes,...]
    all_gather x16 -> x0, blocking collectives: 40.6 us -> none  [carried_in(): everything = jax.tree.map(lambda part: lax.all_gather(part, axis), value)]
    all_to_all x8 -> x0, starting transfers between devices: 32.3 us -> none  [the longest x4 16.2 us: per_device(): lax.all_to_all(ship_bar, 'region', split_axis=0, concat_axis=0, tiled=True)]
    dot_general x17 -> x0, matrix products: 21.3 us -> none  [the longest x4 6.85 us: per_device(): jnp.einsum('ald,dtk->altk', tile_depots, depot_after, precision=highest)]
    unnamed x230 -> x16, local copies, waits for them, and re-layouts: 26.5 us -> 6.42 us
    another operation x8 -> x0, loops' own time: 16.3 us -> none  [carried_in(): return lax.fori_loop(0, peers, hop, start)]
    select_n x32 -> x0, other arithmetic: 16 us -> none  [hop(): return jax.tree.map(lambda a, b: jnp.where(reached, a, b), new, before)]
  transfers between devices with their start and end apart: 8 -> 0, of which waited for: 3 -> 0; matrix products, arithmetic and copies ran while one was open for 13% -> 0% of each run, Pallas kernels for 0% -> 0%
where the time goes in v1:
time: 53.7 us; the launch traced here: 53.4 us
  Pallas kernels  46.3 us (86%)
  local copies, waits for them, and re-layouts  6.42 us (12%)
  between operations  0.67 us (1%)
    pallas_call x1, Pallas kernels, per_device(): pl.pallas_call(functools.partial(kernel, (D, R, S, stores, depots, lanes,...  46.3 us
    unnamed x16, local copies, waits for them, and re-layouts  6.42 us

profile of v1, /device:TPU:1, one launch (start us, length us, event | category | flops | bytes accessed | tf_op | source)
XLA Modules:
  0.0 53.4 jit_solution(4884877384875392065)
XLA Ops:
  0.6 46.3 %shard_map.253 = (f32[512,1,256]{2,1,0:T(1,128)}, f32[100,6,1,256]{3,2,1,0:T(1,128)}, f32[100,6,1,256]{3,2,1,0:T(1,128)}, f32[15,256]{1,0:T(8,128)}, f32[100,6,1,256]{3,2,1,0:T(1,128)}, /*index=5*/f32[15,1,256]{2,1,0:T(1,128)}) custom-call(f32[512,1,256]{2,1,0:T(1,128)} %bitcast.31, f32[100,6,1,256]{3,2,1,0:T(1,128)} %bitcast.24, ...), custom_call_target="tpu_custom_call" | custom-call | tf_op jit(solution)/shard_map/pallas_call | solution.py:550
  47.0 0.0 copy-start.2
  47.0 2.3 %copy.37 = f32[1,1,4,128,1,256]{5,4,3,2,1,0:T(1,128)} copy(f32[1,1,4,128,1,256]{5,4,3,2,1,0:T(1,128)} %bitcast.32) | data formatting | bytes 1048576
  49.2 0.0 copy-done.2
  49.2 0.0 copy-start.1
  49.2 0.8 %copy.38 = f32[1,100,1,6,256]{4,2,3,1,0:T(1,128)} copy(f32[1,100,1,6,256]{4,2,3,1,0:T(1,128)S(1)} %bitcast.29) | data formatting | bytes 1228800
  50.0 0.5 copy-done.1
  50.5 0.0 copy-start.3
  50.5 0.0 copy-start
  50.5 0.8 %copy.39 = f32[1,100,1,6,256]{4,2,3,1,0:T(1,128)} copy(f32[1,100,1,6,256]{4,2,3,1,0:T(1,128)S(1)} %bitcast.28) | data formatting | bytes 1228800
  51.3 0.0 copy-done.3
  51.3 0.6 %copy.40 = f32[15,256]{1,0:T(8,128)} copy(f32[15,256]{1,0:T(8,128)S(1)} %copy-done.3) | data formatting | bytes 30720
  52.0 0.0 copy-done
  52.0 0.0 copy-start.4
  52.0 0.8 %copy.41 = f32[1,100,1,6,256]{4,2,3,1,0:T(1,128)} copy(f32[1,100,1,6,256]{4,2,3,1,0:T(1,128)S(1)} %bitcast.27) | data formatting | bytes 1228800
  52.8 0.0 copy-done.4
  52.8 0.6 %copy.42 = f32[1,15,1,256]{3,2,1,0:T(1,128)} copy(f32[1,15,1,256]{3,2,1,0:T(1,128)S(1)} %bitcast.36) | data formatting | bytes 30720
Async XLA Ops:
  47.0 2.3 %copy-start.2 = (f32[100,6,1,256]{3,2,1,0:T(1,128)S(1)}, f32[100,6,1,256]{3,2,1,0:T(1,128)}, u32[]{:S(2)}) copy-start(f32[100,6,1,256]{3,2,1,0:T(1,128)} %get-tuple-element.13) | copy-start | bytes 1843204
  49.2 1.3 %copy-start.1 = (f32[100,6,1,256]{3,2,1,0:T(1,128)S(1)}, f32[100,6,1,256]{3,2,1,0:T(1,128)}, u32[]{:S(2)}) copy-start(f32[100,6,1,256]{3,2,1,0:T(1,128)} %get-tuple-element.14) | copy-start | bytes 1843204
  50.5 0.8 %copy-start.3 = (f32[15,256]{1,0:T(8,128)S(1)}, f32[15,256]{1,0:T(8,128)}, u32[]{:S(2)}) copy-start(f32[15,256]{1,0:T(8,128)} %get-tuple-element.33) | copy-start | bytes 46084
  50.5 1.4 %copy-start = (f32[100,6,1,256]{3,2,1,0:T(1,128)S(1)}, f32[100,6,1,256]{3,2,1,0:T(1,128)}, u32[]{:S(2)}) copy-start(f32[100,6,1,256]{3,2,1,0:T(1,128)} %get-tuple-element.16) | copy-start | bytes 1843204
  52.0 0.8 %copy-start.4 = (f32[15,1,256]{2,1,0:T(1,128)S(1)}, f32[15,1,256]{2,1,0:T(1,128)}, u32[]{:S(2)}) copy-start(f32[15,1,256]{2,1,0:T(1,128)} %get-tuple-element.17) | copy-start | bytes 46084

commit v2 on v1

--- a/solution.py
+++ b/solution.py
@@ -78,6 +78,9 @@
     keep,
     into_lanes,
     from_lanes,
+    into_sides,
+    from_sides,
+    toll,
     prices,
     bar_high,
     bar_low,
@@ -103,12 +106,20 @@
     out_trecv,
 ):
     D, R, S, stores, depots, lanes, ages, K = sizes
+    assert R & (R - 1) == 0
     SP = round_up(stores, 128)
-    DP = round_up(depots, 8)
+    DP = round_up(depots, 16)
     day, region, scen = lax.axis_index("day"), lax.axis_index("region"), lax.axis_index("scen")
 
     def turn(position, offset, count):
         return lax.rem(position + offset + count, count)
+
+    def partner(x):
+        peer = region
+        for bit in range(R.bit_length() - 1):
+            if x >> bit & 1:
+                peer = peer + (1 << bit) * (1 - 2 * ((region // (1 << bit)) % 2))
+        return peer, peer
 
     def part(which):
         return pl.ds(pl.multiple_of(which * K, K), K)
@@ -126,16 +137,17 @@
     moves = [
         (lambda k: dep_in.at[:, 0, k], lambda t: dep.at[t]),
         (lambda k: supply_in.at[:, 0, k], lambda t: supply.at[t]),
+        (lambda k: bal_in.at[:, 0, 0, k], lambda t: bal.at[t, 0]),
+        (lambda k: dem_in.at[:, 0, k], lambda t: dem.at[t]),
+        (lambda k: short_in.at[:, 0, k], lambda t: short.at[t]),
+        (lambda k: index_in, lambda t: index.at[t]),
     ]
     for a in range(ages):
-        moves.append((lambda k, a=a: bal_in.at[:, a, 0, k], lambda t, a=a: bal.at[t, a]))
-    moves.append((lambda k: dem_in.at[:, 0, k], lambda t: dem.at[t]))
-    for a in range(ages):
+        if a:
+            moves.append((lambda k, a=a: bal_in.at[:, a, 0, k], lambda t, a=a: bal.at[t, a]))
         moves.append((lambda k, a=a: hold_in.at[:, a, 0, k], lambda t, a=a: hold.at[t, a]))
-    for a in range(ages):
         moves.append((lambda k, a=a: sell_in.at[:, a, 0, k], lambda t, a=a: sell.at[t, a]))
-    moves.append((lambda k: short_in.at[:, 0, k], lambda t: short.at[t]))
-    moves.append((lambda k: index_in, lambda t: index.at[t]))
+    first = 3
 
     mine = part(day)
     started = []
@@ -189,11 +201,12 @@
     recvs = []
 
     def exchange(src_of, dst_of, ssem, rsem, dc, dr):
-        to = (turn(day, dc, D), turn(region, dr, R), scen)
+        ahead, behind = partner(dr)
+        to = (turn(day, dc, D), ahead, scen)
         out = to_peer(src_of(to[0], to[1]), dst_of(day, region), ssem, rsem, to)
         out.start()
         sends.append(out)
-        back = (turn(day, -dc, D), turn(region, -dr, R), scen)
+        back = (turn(day, -dc, D), behind, scen)
         return to_peer(src_of(to[0], to[1]), dst_of(back[0], back[1]), ssem, rsem, back)
 
     def ship_tiles(dc, dr):
@@ -206,62 +219,44 @@
             dr,
         )
 
-    ship_recv = []
+    part_recvs = []
+
+    def move(which):
+        for i in which:
+            src, dst = moves[i]
+            for dc in range(1, D):
+                part_recvs.append(
+                    exchange(
+                        lambda t, a: src(part(t)),
+                        lambda t, a: dst(t),
+                        part_send.at[i, dc],
+                        part_recv.at[i, dc],
+                        dc,
+                        0,
+                    )
+                )
+
+    move(range(first))
+    ship_recv = [[ship_tiles(dc, 0) for dc in range(1, D)]]
     for dr in range(1, R):
-        for dc in range(D):
-            ship_recv.append(ship_tiles(dc, dr))
-    part_recvs = []
-    for i, (src, dst) in enumerate(moves):
-        for dc in range(1, D):
-            part_recvs.append(
-                exchange(
-                    lambda t, a, src=src: src(part(t)),
-                    lambda t, a, dst=dst: dst(t),
-                    part_send.at[i, dc],
-                    part_recv.at[i, dc],
-                    dc,
-                    0,
-                )
-            )
-    for dc in range(1, D):
-        ship_recv.append(ship_tiles(dc, 0))
+        ship_recv.append([ship_tiles(dc, dr) for dc in range(D)])
+    move(range(first, len(moves)))
 
     lane_ids = lax.broadcasted_iota(jnp.int32, (lanes, SP), 1).astype(jnp.float32)
-    side_ids = lax.broadcasted_iota(jnp.int32, (lanes, R * DP), 1).astype(jnp.float32)
+    side_ids = lax.broadcasted_iota(jnp.int32, (lanes, DP), 1).astype(jnp.float32)
     store_ids = lax.broadcasted_iota(jnp.int32, (SP, lanes), 0).astype(jnp.float32)
-    depot_ids = lax.broadcasted_iota(jnp.int32, (R * DP, lanes), 0).astype(jnp.float32)
+    depot_ids = lax.broadcasted_iota(jnp.int32, (DP, lanes), 0).astype(jnp.float32)
     volume = volume_ref[:, mine]
     own = pl.ds(region, 1)
-    for a in range(R):
-        rows = slice(a * lanes, (a + 1) * lanes)
-        store_row = lstore_ref[a, own, :].astype(jnp.float32)
-        depot_row = ldepot_ref[a, own, :].astype(jnp.float32) + float(a * DP)
-        weight_row = lmask_ref[a, own, :].astype(jnp.float32)
-        cost_row = cost_ref[a, own, :]
-
-        def column(row):
-            return jnp.broadcast_to(row, (lanes, lanes)).T
-
-        weight = column(weight_row)
-        keep[rows, :] = weight[:, :K]
-        lane_price[rows, :] = column(cost_row)[:, :1] * volume
-        weight = weight[:, :1]
-        into_lanes[rows, 0:SP] = jnp.where(
-            lane_ids == column(store_row)[:, :1], weight, 0.0
-        ).astype(jnp.bfloat16)
-        into_lanes[rows, SP : SP + R * DP] = jnp.where(
-            side_ids == column(depot_row)[:, :1], weight, 0.0
-        ).astype(jnp.bfloat16)
-        from_lanes[0:SP, rows] = jnp.where(store_ids == store_row, weight_row, 0.0).astype(
-            jnp.bfloat16
-        )
-        from_lanes[SP : SP + R * DP, rows] = jnp.where(
-            depot_ids == depot_row, weight_row, 0.0
-        ).astype(jnp.bfloat16)
     prices[...] = jnp.zeros_like(prices)
-
-    for copy in started:
-        copy.wait()
+    for it in range(ITERS):
+        after[it, region] = jnp.zeros((DP, D * K), jnp.float32)
+
+    def local_wait(which):
+        for i in which:
+            started[i].wait()
+
+    local_wait(range(first))
     for copy in part_recvs[: 2 * (D - 1)]:
         copy.wait_recv()
 
@@ -271,10 +266,10 @@
             total = total + dep[t]
         block[it, scen] = total
         later = dep[D - 1]
-        after[it, region, D - 1] = later
+        after[it, region, 0:depots, (D - 1) * K : D * K] = later
         for t in reversed(range(D - 1)):
             later = later + dep[t]
-            after[it, region, t] = later
+            after[it, region, 0:depots, t * K : (t + 1) * K] = later
         waits = []
         for dr in range(1, R):
             waits.append(
@@ -312,23 +307,49 @@
 
     after_recv, block_recv = send_after(0)
 
-    for copy in part_recvs[2 * (D - 1) :]:
+    for a in range(R):
+        rows = slice(a * lanes, (a + 1) * lanes)
+        store_row = lstore_ref[a, own, :].astype(jnp.float32)
+        depot_row = ldepot_ref[a, own, :].astype(jnp.float32)
+        weight_row = lmask_ref[a, own, :].astype(jnp.float32)
+        cost_row = cost_ref[a, own, :]
+
+        def column(row):
+            return jnp.broadcast_to(row, (lanes, lanes)).T
+
+        weight = column(weight_row)
+        keep[rows, :] = weight[:, :K]
+        lane_price[rows, :] = column(cost_row)[:, :1] * volume
+        weight = weight[:, :1]
+        into_lanes[rows, :] = jnp.where(
+            lane_ids == column(store_row)[:, :1], weight, 0.0
+        ).astype(jnp.bfloat16)
+        into_sides[a] = jnp.where(side_ids == column(depot_row)[:, :1], weight, 0.0).astype(
+            jnp.bfloat16
+        )
+        from_lanes[:, rows] = jnp.where(store_ids == store_row, weight_row, 0.0).astype(
+            jnp.bfloat16
+        )
+        from_sides[a] = jnp.where(depot_ids == depot_row, weight_row, 0.0).astype(jnp.bfloat16)
+
+    for copy in part_recvs[2 * (D - 1) : first * (D - 1)]:
         copy.wait_recv()
 
-    pattern_ids = lax.broadcasted_iota(jnp.int32, (pattern.shape[0], stores), 0)
-    table = pattern[...]
-    for t in range(D):
-        chosen = (pattern_ids == index[t]).astype(jnp.float32)
-        demand[t] = (
-            lax.dot_general(
-                chosen,
-                table,
-                (((0,), (0,)), ((), ())),
-                precision=lax.Precision.HIGHEST,
-                preferred_element_type=jnp.float32,
+    def set_demand():
+        pattern_ids = lax.broadcasted_iota(jnp.int32, (pattern.shape[0], stores), 0)
+        table = pattern[...]
+        for t in range(D):
+            chosen = (pattern_ids == index[t]).astype(jnp.float32)
+            demand[t] = (
+                lax.dot_general(
+                    chosen,
+                    table,
+                    (((0,), (0,)), ((), ())),
+                    precision=lax.Precision.HIGHEST,
+                    preferred_element_type=jnp.float32,
+                )
+                * base[...]
             )
-            * base[...]
-        )
 
     hcost = hcost_ref[:, mine]
     unit_price = price_ref[:, mine]
@@ -398,21 +419,7 @@
         final = it == ITERS - 1
         for t in range(D):
             prices[0:stores, t * K : (t + 1) * K] = bal[t, 0]
-        early = D if it == 0 or final else 1
-        for t in range(early):
-            step_stores(t)
-        if final:
-            put_ages(0, hold, hold_out, range(ages))
-            put_ages(ages, sell, sell_out, range(ages))
-            put_ages(2 * ages, bal, bal_out, range(1, ages))
-        if it == 0:
-            for copy in ship_recv:
-                copy.wait_recv()
-        for copy in after_recv:
-            copy.wait_recv()
-        for a in range(R):
-            for t in range(D):
-                prices[SP + a * DP : SP + a * DP + depots, t * K : (t + 1) * K] = after[it, a, t]
+        early = D if final else 0 if it == 0 else 1
         high, low = split_bf16(prices[...])
         for a in range(R):
             rows = slice(a * lanes, (a + 1) * lanes)
@@ -420,32 +427,55 @@
             cost = dot(spread, high) + dot(spread, low)
             for t in range(D):
                 cols = slice(t * K, (t + 1) * K)
+                toll[rows, cols] = lane_price[rows, :] + cost[:, cols]
+        for t in range(early):
+            step_stores(t)
+        if final:
+            put_ages(0, hold, hold_out, range(ages))
+            put_ages(ages, sell, sell_out, range(ages))
+            put_ages(2 * ages, bal, bal_out, range(1, ages))
+        flow_waits = []
+        for x in range(R):
+            a = partner(x)[1]
+            if it == 0:
+                for copy in ship_recv[x]:
+                    copy.wait_recv()
+                if x == 0:
+                    local_wait([len(moves) + len(extra)])
+            if x:
+                after_recv[x - 1].wait_recv()
+            rows = tile(a)
+            high, low = split_bf16(after[it, a])
+            spread = into_sides[a]
+            cost = dot(spread, high) + dot(spread, low)
+            weight = keep[rows, :]
+            bars = []
+            for t in range(D):
+                cols = slice(t * K, (t + 1) * K)
                 old = ship[rows, cols]
-                new = keep[rows, :] * jnp.maximum(
-                    0.0, old - primal_step * (lane_price[rows, :] + cost[:, cols])
+                new = weight * jnp.maximum(
+                    0.0, old - primal_step * (toll[rows, cols] + cost[:, cols])
                 )
                 ship[rows, cols] = new
-                bar = split_bf16(2.0 * new - old)
-                bar_high[rows, cols] = bar[0]
-                bar_low[rows, cols] = bar[1]
-        gather = from_lanes[SP:, :]
-        flow = dot(gather, bar_high[...]) + dot(gather, bar_low[...])
-        for a in range(R):
-            flow_send[it, a] = flow[a * DP : (a + 1) * DP, :]
-        flow_waits = []
-        for dr in range(1, R):
-            flow_waits.append(
-                exchange(
-                    lambda t, a: flow_send.at[it, a],
-                    lambda t, a: flow_recv.at[it, dr],
-                    flow_ssem.at[it, dr],
-                    flow_rsem.at[it, dr],
-                    0,
-                    dr,
+                bars.append(2.0 * new - old)
+            high, low = split_bf16(jnp.concatenate(bars, axis=1))
+            bar_high[rows, :] = high
+            bar_low[rows, :] = low
+            gather = from_sides[a]
+            flow_send[it, a] = dot(gather, high) + dot(gather, low)
+            if x:
+                flow_waits.append(
+                    exchange(
+                        lambda t, a: flow_send.at[it, a],
+                        lambda t, a: flow_recv.at[it, x],
+                        flow_ssem.at[it, x],
+                        flow_rsem.at[it, x],
+                        0,
+                        x,
+                    )
                 )
-            )
         if final:
-            for dr in list(range(1, R)) + [0]:
+            for dr in list(range(R - 1, 0, -1)) + [0]:
                 for dc in range(D):
                     if dc == 0 and dr == 0:
                         local = pltpu.make_async_copy(
@@ -466,9 +496,14 @@
                             dr,
                         )
                     )
+        if it == 0:
+            local_wait(range(first, len(moves) + len(extra)))
+            for copy in part_recvs[first * (D - 1) :]:
+                copy.wait_recv()
+            set_demand()
         for t in range(early, D):
             step_stores(t)
-        gather = from_lanes[0:SP, :]
+        gather = from_lanes[...]
         arrivals = dot(gather, bar_high[...]) + dot(gather, bar_low[...])
         for t in range(D):
             bal[t, 0] = bal[t, 0] + dual_step * arrivals[0:stores, t * K : (t + 1) * K]
@@ -541,7 +576,7 @@
     K = items // D
     f32 = jnp.float32
     SP = round_up(stores, 128)
-    DP = round_up(depots, 8)
+    DP = round_up(depots, 16)
     any_ = pl.BlockSpec(memory_space=pl.ANY)
     vmem = pl.BlockSpec(memory_space=pltpu.VMEM)
     moved = 4 + 3 * ages + 1
@@ -577,14 +612,17 @@
             pltpu.VMEM((D, depots, K), f32),
             pltpu.VMEM((rows, K), f32),
             pltpu.VMEM((rows, K), f32),
-            pltpu.VMEM((rows, SP + R * DP), jnp.bfloat16),
-            pltpu.VMEM((SP + R * DP, rows), jnp.bfloat16),
-            pltpu.VMEM((SP + R * DP, D * K), f32),
+            pltpu.VMEM((rows, SP), jnp.bfloat16),
+            pltpu.VMEM((SP, rows), jnp.bfloat16),
+            pltpu.VMEM((R, lanes, DP), jnp.bfloat16),
+            pltpu.VMEM((R, DP, lanes), jnp.bfloat16),
+            pltpu.VMEM((rows, D * K), f32),
+            pltpu.VMEM((SP, D * K), f32),
             pltpu.VMEM((rows, D * K), jnp.bfloat16),
             pltpu.VMEM((rows, D * K), jnp.bfloat16),
             pltpu.VMEM((ITERS, R, DP, D * K), f32),
             pltpu.VMEM((ITERS, R, DP, D * K), f32),
-            pltpu.VMEM((ITERS, R, D, depots, K), f32),
+            pltpu.VMEM((ITERS, R, DP, D * K), f32),
             pltpu.VMEM((ITERS, S, depots, K), f32),
             DMA((moved + 5,)),
             DMA((moved, D)),

time: 53.7 us -> 52.7 us (0.981)
  Pallas kernels: 46.3 us -> 45.3 us
    pallas_call x1, Pallas kernels: 46.3 us -> 45.3 us  [per_device(): pl.pallas_call(functools.partial(kernel, (D, R, S, stores, depots, lanes,...]
where the time goes in v2:
time: 52.7 us; the launch traced here: 52.4 us
  Pallas kernels  45.3 us (86%)
  local copies, waits for them, and re-layouts  6.42 us (12%)
  between operations  0.67 us (1%)
    pallas_call x1, Pallas kernels, per_device(): pl.pallas_call(functools.partial(kernel, (D, R, S, stores, depots, lanes,...  45.3 us
    unnamed x16, local copies, waits for them, and re-layouts  6.42 us

profile of v2, /device:TPU:1, one launch (start us, length us, event | category | flops | bytes accessed | tf_op | source)
XLA Modules:
  0.0 52.4 jit_solution(13513349583712115727)
XLA Ops:
  0.6 45.3 %shard_map.253 = (f32[512,1,256]{2,1,0:T(1,128)}, f32[100,6,1,256]{3,2,1,0:T(1,128)}, f32[100,6,1,256]{3,2,1,0:T(1,128)}, f32[15,256]{1,0:T(8,128)}, f32[100,6,1,256]{3,2,1,0:T(1,128)}, /*index=5*/f32[15,1,256]{2,1,0:T(1,128)}) custom-call(f32[512,1,256]{2,1,0:T(1,128)} %bitcast.31, f32[100,6,1,256]{3,2,1,0:T(1,128)} %bitcast.24, ...), custom_call_target="tpu_custom_call" | custom-call | tf_op jit(solution)/shard_map/pallas_call | solution.py:585
  46.0 0.0 copy-start.2
  46.0 2.3 %copy.37 = f32[1,1,4,128,1,256]{5,4,3,2,1,0:T(1,128)} copy(f32[1,1,4,128,1,256]{5,4,3,2,1,0:T(1,128)} %bitcast.32) | data formatting | bytes 1048576
  48.3 0.0 copy-done.2
  48.3 0.0 copy-start.1
  48.3 0.8 %copy.38 = f32[1,100,1,6,256]{4,2,3,1,0:T(1,128)} copy(f32[1,100,1,6,256]{4,2,3,1,0:T(1,128)S(1)} %bitcast.29) | data formatting | bytes 1228800
  49.1 0.5 copy-done.1
  49.6 0.0 copy-start.3
  49.6 0.0 copy-start
  49.6 0.8 %copy.39 = f32[1,100,1,6,256]{4,2,3,1,0:T(1,128)} copy(f32[1,100,1,6,256]{4,2,3,1,0:T(1,128)S(1)} %bitcast.28) | data formatting | bytes 1228800
  50.4 0.0 copy-done.3
  50.4 0.6 %copy.40 = f32[15,256]{1,0:T(8,128)} copy(f32[15,256]{1,0:T(8,128)S(1)} %copy-done.3) | data formatting | bytes 30720
  51.0 0.0 copy-done
  51.0 0.0 copy-start.4
  51.0 0.8 %copy.41 = f32[1,100,1,6,256]{4,2,3,1,0:T(1,128)} copy(f32[1,100,1,6,256]{4,2,3,1,0:T(1,128)S(1)} %bitcast.27) | data formatting | bytes 1228800
  51.8 0.0 copy-done.4
  51.8 0.6 %copy.42 = f32[1,15,1,256]{3,2,1,0:T(1,128)} copy(f32[1,15,1,256]{3,2,1,0:T(1,128)S(1)} %bitcast.36) | data formatting | bytes 30720
Async XLA Ops:
  46.0 2.3 %copy-start.2 = (f32[100,6,1,256]{3,2,1,0:T(1,128)S(1)}, f32[100,6,1,256]{3,2,1,0:T(1,128)}, u32[]{:S(2)}) copy-start(f32[100,6,1,256]{3,2,1,0:T(1,128)} %get-tuple-element.13) | copy-start | bytes 1843204
  48.3 1.3 %copy-start.1 = (f32[100,6,1,256]{3,2,1,0:T(1,128)S(1)}, f32[100,6,1,256]{3,2,1,0:T(1,128)}, u32[]{:S(2)}) copy-start(f32[100,6,1,256]{3,2,1,0:T(1,128)} %get-tuple-element.14) | copy-start | bytes 1843204
  49.6 0.8 %copy-start.3 = (f32[15,256]{1,0:T(8,128)S(1)}, f32[15,256]{1,0:T(8,128)}, u32[]{:S(2)}) copy-start(f32[15,256]{1,0:T(8,128)} %get-tuple-element.33) | copy-start | bytes 46084
  49.6 1.4 %copy-start = (f32[100,6,1,256]{3,2,1,0:T(1,128)S(1)}, f32[100,6,1,256]{3,2,1,0:T(1,128)}, u32[]{:S(2)}) copy-start(f32[100,6,1,256]{3,2,1,0:T(1,128)} %get-tuple-element.16) | copy-start | bytes 1843204
  51.0 0.8 %copy-start.4 = (f32[15,1,256]{2,1,0:T(1,128)S(1)}, f32[15,1,256]{2,1,0:T(1,128)}, u32[]{:S(2)}) copy-start(f32[15,1,256]{2,1,0:T(1,128)} %get-tuple-element.17) | copy-start | bytes 46084
